TPU v7x, 128 devices: a whole 4x4x4 slice. The times are simulated.
128 devices in a mesh: row: 8 (over x, core), col: 16 (over z, y).
Axes of the slice: x: 4, y: 4, z: 4, core: 2. Of those that a mesh axis runs over, the one named last changes fastest.
Arguments:
- ham: bfloat16 [6144, 6144], P('row', 'col'), may hold values from -0.078125 to 0.078125
- deriv: bfloat16 [6144, 6144], P('row', 'col'), may hold values from -6 to 6
- band: int32 [48], replicated, may hold values from 1 to 24, as said below
- frag_of: int32 [48], replicated, may hold values from 0 to 31
Outputs:
- sign_iterate: bfloat16 [6144, 6144], P('row', 'col')
- energy_density: bfloat16 [6144, 6144], P('row', 'col')
- pulay_terms: float32 [32, 128], P('col')
Inputs may be any that keep to these rules, and one draw needn't show every extreme that they name: Some block row has band half-width exactly 24.
All inputs are finite; a program needn't handle non-finite values.
Results may differ from a plain program's by a relative error of at most 0.006.
Values may be sent and summed in bfloat16 or wider, within the bound.
A program may use at most 64 MiB of HBM per device.

v0:
```python
import jax
import jax.numpy as jnp
from jax import lax
from jax.sharding import PartitionSpec as P

BLK = 128
FRAG_DEV = 2


def column_panel_of(right_matrix):
    return lax.all_gather(right_matrix, "row", axis=0, tiled=True)


def folded_product(left_matrix, right_matrix):
    whole_panel = column_panel_of(right_matrix)
    return jnp.dot(
        lax.all_gather(left_matrix, "col", axis=1, tiled=True),
        whole_panel,
        preferred_element_type=jnp.float32,
    )


def body(ham, deriv, band, frag_of):
    rows_here = ham.shape[0]
    cols_here = ham.shape[1]
    block_rows = rows_here // BLK
    block_cols = cols_here // BLK
    row_index = lax.axis_index("row")
    col_index = lax.axis_index("col")
    row_blocks = row_index * block_rows + jnp.arange(block_rows, dtype=jnp.int32)
    col_blocks = col_index * block_cols + jnp.arange(block_cols, dtype=jnp.int32)
    row_band = lax.dynamic_slice_in_dim(band, row_index * block_rows, block_rows)
    col_band = lax.dynamic_slice_in_dim(band, col_index * block_cols, block_cols)
    widest = jnp.maximum(row_band[:, None], col_band[None, :])
    inside = jnp.abs(row_blocks[:, None] - col_blocks[None, :]) <= widest
    pattern = jnp.repeat(jnp.repeat(inside.astype(jnp.float32), BLK, axis=0), BLK, axis=1)
    global_rows = row_index * rows_here + jnp.arange(rows_here, dtype=jnp.int32)
    global_cols = col_index * cols_here + jnp.arange(cols_here, dtype=jnp.int32)
    identity = (global_rows[:, None] == global_cols[None, :]).astype(jnp.float32)
    start = (ham.astype(jnp.float32) * pattern).astype(jnp.bfloat16)

    def start_times(right_matrix):
        return folded_product(start, right_matrix)

    square = (start_times(start) * pattern).astype(jnp.bfloat16)
    cubic = start_times(square)
    sign_iterate = (pattern * (1.5 * start.astype(jnp.float32) - 0.5 * cubic)).astype(jnp.bfloat16)
    density = (0.5 * (identity - sign_iterate.astype(jnp.float32))).astype(jnp.bfloat16)
    weighted = (start_times(density) * pattern).astype(jnp.bfloat16)
    energy_density = (folded_product(density, weighted) * pattern).astype(jnp.bfloat16)
    column_terms = jnp.sum(energy_density.astype(jnp.float32) * deriv.astype(jnp.float32), axis=0)
    column_terms = column_terms.reshape(block_cols, BLK)
    local_frags = lax.dynamic_slice_in_dim(frag_of, col_index * block_cols, block_cols)
    fragment_count = FRAG_DEV * lax.axis_size("col")
    fragments = jnp.arange(fragment_count, dtype=jnp.int32)
    onehot = (local_frags[None, :] == fragments[:, None]).astype(jnp.float32)
    partial_value = jnp.dot(onehot, column_terms, precision=lax.Precision.HIGHEST)
    grand_total = lax.psum(partial_value, ("row", "col"))
    pulay_terms = lax.dynamic_slice_in_dim(grand_total, col_index * FRAG_DEV, FRAG_DEV, 0)
    return (sign_iterate, energy_density, pulay_terms)


def solution(mesh):
    placed = (P("row", "col"), P("row", "col"), P(), P())
    return jax.shard_map(
        body,
        mesh=mesh,
        in_specs=placed,
        out_specs=(P("row", "col"), P("row", "col"), P("col", None)),
        check_vma=False,
    )
```

profile of v0, /device:TPU:1, one launch (start us, length us, event | category | flops | bytes accessed | tf_op | source)
XLA Modules:
  0.0 432.5 jit_solution(7368020755092818838)
XLA Ops:
  7.2 0.0 all-gather.9.cloned.1.call-start
  7.2 0.7 dynamic_slice.13
  8.0 0.7 dynamic_slice.12
  8.7 0.1 fusion.9
  8.8 0.1 broadcast_bitcast_fusion
  8.9 0.1 broadcast_in_dim.5
  9.0 0.0 copy-start
  9.0 0.4 copy.8
  9.3 0.7 copy-done
  10.0 0.9 multiply_convert_fusion.1
  11.0 0.0 all-gather.9.cloned.1.call-update
  11.0 0.0 all-gather.7.cloned.1.call-start
  11.0 0.7 all-gather.7.cloned.1.call-update
  11.7 0.0 all-gather.11.cloned.1.call-start
  11.8 37.2 %all-gather.9.cloned.1.call-done = bf16[6144,384]{1,0:T(8,128)(2,1)} async-done(((bf16[768,384]{1,0:T(8,128)(2,1)}), bf16[6144,384]{1,0:T(8,128)(2,1)}) %all-gather.9.cloned.1.call-update) | async-done | bytes 4718608 | tf_op jit(solution)/shard_map/all_gather | solution.py:11
  48.9 83.6 %all-gather.7.cloned.1.call-done = bf16[768,6144]{1,0:T(8,128)(2,1)} async-done(((bf16[768,384]{1,0:T(8,128)(2,1)}), bf16[768,6144]{1,0:T(8,128)(2,1)}) %all-gather.7.cloned.1.call-update) | async-done | bytes 9437200 | tf_op jit(solution)/shard_map/all_gather | solution.py:17
  132.5 9.7 %fusion.3 = bf16[768,384]{0,1:T(8,128)(2,1)} fusion(f32[768,384]{0,1:T(8,128)S(1)} %bitcast.20, bf16[768,6144]{1,0:T(8,128)(2,1)} %all-gather.7.cloned.1.call-done, bf16[6144,384]{1,0:T(8,128)(2,1)} %all-gather.9.cloned.1.call-done), kind=kOutput, calls=%fused_computation.7 | convolution fusion | flops 3624468480 | bytes 15925248 | tf_op jit(solution)/shard_map/dot_general | solution.py:16
  142.2 0.0 all-gather.11.cloned.1.call-update
  142.3 0.0 all-gather.15.cloned.1.call-start
  142.3 35.3 %all-gather.11.cloned.1.call-done = bf16[6144,384]{0,1:T(8,128)(2,1)} async-done(((bf16[768,384]{0,1:T(8,128)(2,1)}), bf16[6144,384]{0,1:T(8,128)(2,1)}) %all-gather.11.cloned.1.call-update) | async-done | bytes 4718608 | tf_op jit(solution)/shard_map/all_gather | solution.py:11
  177.6 10.0 %multiply_convert_fusion = (bf16[768,384]{1,0:T(8,128)(2,1)}, bf16[768,384]{1,0:T(8,128)(2,1)}) fusion(s32[384]{0:T(512)S(1)} %iota_add_fusion.1, s32[768]{0:T(1024)S(1)} %iota_add_fusion, f32[768,384]{1,0:T(8,128)S(1)} %copy.8, bf16[768,6144]{1,0:T(8,128)(2,1)} %all-gather.7.cloned.1.call-done, bf16[6144,384]{0,1:T(8,128)(2,1)} %all-gather.11.cloned.1.call-done, ...), kind=kOutput, calls=%fused_computation.11 | convolution fusion | flops 3628302336 | bytes 17109504 | tf_op jit(solution)/shard_map/dot_general | solution.py:16
  187.6 0.0 all-gather.15.cloned.1.call-update
  187.6 0.0 all-gather.17.cloned.1.call-start
  187.7 34.3 %all-gather.15.cloned.1.call-done = bf16[6144,384]{1,0:T(8,128)(2,1)} async-done(((bf16[768,384]{1,0:T(8,128)(2,1)}), bf16[6144,384]{1,0:T(8,128)(2,1)}) %all-gather.15.cloned.1.call-update) | async-done | bytes 4718608 | tf_op jit(solution)/shard_map/all_gather | solution.py:11
  222.0 9.7 %fusion.4 = bf16[768,384]{0,1:T(8,128)(2,1)} fusion(f32[768,384]{0,1:T(8,128)S(1)} %bitcast.21, bf16[768,6144]{1,0:T(8,128)(2,1)} %all-gather.7.cloned.1.call-done, bf16[6144,384]{1,0:T(8,128)(2,1)} %all-gather.15.cloned.1.call-done), kind=kOutput, calls=%fused_computation.8 | convolution fusion | flops 3624468480 | bytes 15925248 | tf_op jit(solution)/shard_map/dot_general | solution.py:16
  231.7 0.0 copy-start.2
  231.7 0.0 copy-start.1
  231.7 0.0 all-gather.17.cloned.1.call-update
  231.7 0.2 all-gather.13.cloned.1.call-start
  231.9 0.3 all-gather.13.cloned.1.call-update
  232.3 0.0 copy-done.2
  232.3 0.1 dynamic_slice.14
  232.4 33.7 %all-gather.17.cloned.1.call-done = bf16[6144,384]{0,1:T(8,128)(2,1)} async-done(((bf16[768,384]{0,1:T(8,128)(2,1)}), bf16[6144,384]{0,1:T(8,128)(2,1)}) %all-gather.17.cloned.1.call-update) | async-done | bytes 4718608 | tf_op jit(solution)/shard_map/all_gather | solution.py:11
  266.1 83.4 %all-gather.13.cloned.1.call-done = bf16[768,6144]{1,0:T(8,128)(2,1)} async-done(((bf16[768,384]{1,0:T(8,128)(2,1)}), bf16[768,6144]{1,0:T(8,128)(2,1)}) %all-gather.13.cloned.1.call-update) | async-done | bytes 9437200 | tf_op jit(solution)/shard_map/all_gather | solution.py:17
  349.5 0.0 copy-done.1
  349.5 9.8 %multiply_reduce_fusion = (f32[384]{0:T(512)S(1)}, bf16[768,384]{1,0:T(8,128)(2,1)}) fusion(bf16[768,384]{1,0:T(8,128)(2,1)S(1)} %copy-done.1, f32[768,384]{1,0:T(8,128)S(1)} %copy.8, bf16[768,6144]{1,0:T(8,128)(2,1)} %all-gather.13.cloned.1.call-done, bf16[6144,384]{0,1:T(8,128)(2,1)} %all-gather.17.cloned.1.call-done), kind=kOutput, calls=%fused_computation.10 | convolution fusion | flops 3625647616 | bytes 16516608 | tf_op jit(solution)/shard_map/dot_general | solution.py:16
  359.3 0.1 fusion.6
  359.4 65.7 %psum.7 = f32[32,128]{1,0:T(8,128)S(1)} all-reduce(f32[32,128]{1,0:T(8,128)S(1)} %fusion.6), channel_id=1, replica_groups=mesh['row'=8,'col'=16] {'row','col'}, use_global_device_ids=true, to_apply=%region_1.0 | all-reduce | flops 4096 | bytes 32768 | tf_op jit(solution)/shard_map/psum | solution.py:58
  425.1 0.6 constant_dynamic-slice_fusion
  (5 shorter events, 0.0 us)
Async XLA Ops:
  7.2 41.8 %all-gather.9.cloned.1.call-start = ((), (), s32[]{:S(2)}) async-start(), calls=%async_computation.1 | async-start | bytes 5308416 | tf_op jit(solution)/shard_map/all_gather | solution.py:11
  9.0 1.1 copy-start
  11.0 121.6 %all-gather.7.cloned.1.call-start = ((), (), s32[]{:S(2)}) async-start(), calls=%async_computation | async-start | bytes 10027008 | tf_op jit(solution)/shard_map/all_gather | solution.py:17
  11.7 165.9 %all-gather.11.cloned.1.call-start = ((), (), s32[]{:S(2)}) async-start(), calls=%async_computation.2 | async-start | bytes 5308416 | tf_op jit(solution)/shard_map/all_gather | solution.py:11
  142.3 79.7 %all-gather.15.cloned.1.call-start = ((), (), s32[]{:S(2)}) async-start(), calls=%async_computation.4 | async-start | bytes 5308416 | tf_op jit(solution)/shard_map/all_gather | solution.py:11
  187.6 78.5 %all-gather.17.cloned.1.call-start = ((), (), s32[]{:S(2)}) async-start(), calls=%async_computation.5 | async-start | bytes 5308416 | tf_op jit(solution)/shard_map/all_gather | solution.py:11
  231.7 0.7 copy-start.2
  231.7 117.8 %copy-start.1 = (bf16[768,384]{1,0:T(8,128)(2,1)S(1)}, bf16[768,384]{1,0:T(8,128)(2,1)}, u32[]{:S(2)}) copy-start(bf16[768,384]{1,0:T(8,128)(2,1)} %param.5) | copy-start | bytes 1769476
  231.7 117.8 %all-gather.13.cloned.1.call-start = ((), (), s32[]{:S(2)}) async-start(), calls=%async_computation.3 | async-start | bytes 10027008 | tf_op jit(solution)/shard_map/all_gather | solution.py:17
Sparse Core Ops, SparseCore 0:
  11.1 37.7 all-gather.8
  51.6 80.8 all-gather.6
  142.4 35.1 all-gather.10
  187.7 34.2 all-gather.14
  231.8 34.2 all-gather.16
  268.6 80.8 all-gather.12
where the time goes:
time: 433 us
  waiting for transfers between devices  309 us (71%)
  blocking collectives  65.7 us (15%)
  matrix products  39.3 us (9%)
  between operations  14.2 us (3%)
    all_gather x2, waiting for transfers between devices, folded_product(): lax.all_gather(left_matrix, 'col', axis=1, tiled=True)  167 us
    all_gather x4, waiting for transfers between devices, column_panel_of(): return lax.all_gather(right_matrix, 'row', axis=0, tiled=True)  140 us
    psum x1, blocking collectives, body(): grand_total = lax.psum(partial_value, ('row', 'col'))  65.7 us
    dot_general x4, matrix products, folded_product(): jnp.dot(lax.all_gather(left_matrix, 'col', axis=1, tiled=True), whole_pan...  39.1 us
  transfers between devices with their start and end apart: 6, of which 6 were waited for; matrix products, arithmetic and copies ran while one was open for 0% of the time, Pallas kernels for 0%

commit v1 on v0

--- a/solution.py
+++ b/solution.py
@@ -1,10 +1,27 @@
+import functools
 import jax
 import jax.numpy as jnp
 from jax import lax
 from jax.sharding import PartitionSpec as P
+from jax.lax import all_to_all, axis_size
 
 BLK = 128
 FRAG_DEV = 2
+
+
+def _attach_files(message, group_axis):
+    return jnp.concatenate(
+        all_to_all(
+            jnp.stack(axis_size(group_axis) * [message], axis=0),
+            axis_name=group_axis,
+            split_axis=0,
+            concat_axis=0,
+        ),
+        1,
+    )
+
+
+points_run = functools.partial(_attach_files, group_axis="col")
 
 
 def column_panel_of(right_matrix):
@@ -13,11 +30,7 @@
 
 def folded_product(left_matrix, right_matrix):
     whole_panel = column_panel_of(right_matrix)
-    return jnp.dot(
-        lax.all_gather(left_matrix, "col", axis=1, tiled=True),
-        whole_panel,
-        preferred_element_type=jnp.float32,
-    )
+    return jnp.dot(points_run(left_matrix), whole_panel, preferred_element_type=jnp.float32)
 
 
 def body(ham, deriv, band, frag_of):

time: 433 us -> 452 us (1.044)
  starting transfers between devices: 0.42 us -> 15.7 us
  local copies, waits for them, and re-layouts: 3.37 us -> 14.1 us
    all_to_all x0 -> x2, waiting for transfers between devices: none -> 209 us  [_attach_files(): all_to_all(jnp.stack(axis_size(group_axis) * [message], axis=0), axis_nam...]
    all_gather x2 -> x0, waiting for transfers between devices: 167 us -> none  [folded_product(): lax.all_gather(left_matrix, 'col', axis=1, tiled=True)]
    all_gather x4, waiting for transfers between devices: 140 us -> 95.7 us  [column_panel_of(): return lax.all_gather(right_matrix, 'row', axis=0, tiled=True)]
    all_to_all x0 -> x2, starting transfers between devices: none -> 15.4 us  [_attach_files(): all_to_all(jnp.stack(axis_size(group_axis) * [message], axis=0), axis_nam...]
    another operation x0 -> x2, local copies, waits for them, and re-layouts: none -> 9.2 us  [_attach_files(): jnp.stack(axis_size(group_axis) * [message], axis=0)]
  transfers between devices with their start and end apart: 6 -> 6, of which waited for: 6 -> 5; matrix products, arithmetic and copies ran while one was open for 0% -> 3% of each run, Pallas kernels for 0% -> 0%
where the time goes in v1:
time: 452 us
  waiting for transfers between devices  305 us (67%)
  blocking collectives  63.2 us (14%)
  matrix products  39.5 us (9%)
  starting transfers between devices  15.7 us (3%)
  local copies, waits for them, and re-layouts  14.1 us (3%)
  between operations  13.9 us (3%)
    all_to_all x2, waiting for transfers between devices, _attach_files(): all_to_all(jnp.stack(axis_size(group_axis) * [message], axis=0), axis_nam...  209 us
    all_gather x4, waiting for transfers between devices, column_panel_of(): return lax.all_gather(right_matrix, 'row', axis=0, tiled=True)  95.7 us
    psum x1, blocking collectives, body(): grand_total = lax.psum(partial_value, ('row', 'col'))  63.2 us
    dot_general x4, matrix products, folded_product(): jnp.dot(points_run(left_matrix), whole_panel, preferred_element_type=jnp....  39.4 us
    all_to_all x2, starting transfers between devices, _attach_files(): all_to_all(jnp.stack(axis_size(group_axis) * [message], axis=0), axis_nam...  15.4 us
    another operation x2, local copies, waits for them, and re-layouts, _attach_files(): jnp.stack(axis_size(group_axis) * [message], axis=0)  9.2 us
  transfers between devices with their start and end apart: 6, of which 5 were waited for; matrix products, arithmetic and copies ran while one was open for 3% of the time, Pallas kernels for 0%

profile of v1, /device:TPU:1, one launch (start us, length us, event | category | flops | bytes accessed | tf_op | source)
XLA Modules:
  0.0 451.7 jit_solution(11445016482214334087)
XLA Ops:
  7.2 0.7 dynamic_slice.13
  7.9 0.7 dynamic_slice.12
  8.7 0.1 fusion.9
  8.7 0.1 broadcast_bitcast_fusion
  8.8 0.1 broadcast_in_dim.5
  8.9 0.0 copy-start.1
  8.9 0.4 copy.9
  9.3 0.7 copy-done.1
  10.0 0.1 multiply_convert_fusion.1
  10.1 0.0 copy-start
  10.1 0.3 copy.8
  10.4 4.6 %stack.4 = bf16[16,768,384]{1,2,0:T(8,128)(2,1)} broadcast(bf16[768,384]{0,1:T(8,128)(2,1)S(1)} %copy.8), dimensions={1,2} | broadcast | bytes 10027008 | tf_op jit(solution)/shard_map/stack | solution.py:15
  14.9 0.0 copy-done
  14.9 8.6 %all-to-all-start = ((bf16[16,768,384]{1,2,0:T(8,128)(2,1)}), bf16[16,768,384]{1,2,0:T(8,128)(2,1)}, u32[]{:S(2)}, u32[]{:S(2)}) async-start(bf16[16,768,384]{1,2,0:T(8,128)(2,1)} %stack.4), calls=%async_computation | async-start | bytes 18874368 | tf_op jit(solution)/shard_map/all_to_all | solution.py:14
  23.6 0.0 all-gather.5.cloned.1.call-start
  23.6 0.7 all-gather.5.cloned.1.call-update
  24.3 0.0 all-gather.7.cloned.1.call-start
  24.4 38.7 %all-gather.5.cloned.1.call-done = bf16[6144,384]{1,0:T(8,128)(2,1)} async-done(((bf16[768,384]{1,0:T(8,128)(2,1)}), bf16[6144,384]{1,0:T(8,128)(2,1)}) %all-gather.5.cloned.1.call-update) | async-done | bytes 4718608 | tf_op jit(solution)/shard_map/all_gather | solution.py:28
  63.1 99.4 %all-to-all-done = bf16[16,768,384]{1,2,0:T(8,128)(2,1)} async-done(((bf16[16,768,384]{1,2,0:T(8,128)(2,1)}), bf16[16,768,384]{1,2,0:T(8,128)(2,1)}, u32[]{:S(2)}, u32[]{:S(2)}) %all-to-all-start) | async-done | bytes 9437216 | tf_op jit(solution)/shard_map/all_to_all | solution.py:14
  162.5 0.0 copy-start.2
  162.5 9.8 %fusion = bf16[768,384]{0,1:T(8,128)(2,1)} fusion(f32[768,384]{0,1:T(8,128)S(1)} %bitcast.26, bf16[768,6144]{0,1:T(8,128)(2,1)} %bitcast.2, bf16[6144,384]{1,0:T(8,128)(2,1)} %all-gather.5.cloned.1.call-done), kind=kOutput, calls=%fused_computation.4 | convolution fusion | flops 3624468480 | bytes 15925248 | tf_op jit(solution)/shard_map/dot_general | solution.py:33
  172.3 0.0 all-gather.7.cloned.1.call-update
  172.4 0.0 all-gather.9.cloned.1.call-start
  172.4 35.5 %all-gather.7.cloned.1.call-done = bf16[6144,384]{0,1:T(8,128)(2,1)} async-done(((bf16[768,384]{0,1:T(8,128)(2,1)}), bf16[6144,384]{0,1:T(8,128)(2,1)}) %all-gather.7.cloned.1.call-update) | async-done | bytes 4718608 | tf_op jit(solution)/shard_map/all_gather | solution.py:28
  208.0 0.0 copy-done.2
  208.0 10.1 %multiply_convert_fusion = (bf16[768,384]{1,0:T(8,128)(2,1)}, bf16[768,384]{1,0:T(8,128)(2,1)}) fusion(s32[384]{0:T(512)S(1)} %iota_add_fusion.1, s32[768]{0:T(1024)S(1)} %iota_add_fusion, f32[768,384]{1,0:T(8,128)S(1)} %copy.9, bf16[768,6144]{0,1:T(8,128)(2,1)} %bitcast.2, bf16[6144,384]{0,1:T(8,128)(2,1)} %all-gather.7.cloned.1.call-done, ...), kind=kOutput, calls=%fused_computation.11 | convolution fusion | flops 3628302336 | bytes 17109504 | tf_op jit(solution)/shard_map/dot_general | solution.py:33
  218.1 0.0 all-gather.9.cloned.1.call-update
  218.1 1.3 copy.10
  219.4 4.6 %stack.5 = bf16[16,768,384]{1,2,0:T(8,128)(2,1)} broadcast(bf16[768,384]{0,1:T(8,128)(2,1)S(1)} %copy.10), dimensions={1,2} | broadcast | bytes 10027008 | tf_op jit(solution)/shard_map/stack | solution.py:15
  224.0 6.7 %all-to-all-start.1 = ((bf16[16,768,384]{1,2,0:T(8,128)(2,1)}), bf16[16,768,384]{1,2,0:T(8,128)(2,1)}, u32[]{:S(2)}, u32[]{:S(2)}) async-start(bf16[16,768,384]{1,2,0:T(8,128)(2,1)} %stack.5), calls=%async_computation.1 | async-start | bytes 18874368 | tf_op jit(solution)/shard_map/all_to_all | solution.py:14
  230.8 0.0 copy-start.4
  230.8 0.0 copy-start.3
  230.8 0.2 all-gather.11.cloned.1.call-start
  231.0 21.4 %all-gather.9.cloned.1.call-done = bf16[6144,384]{1,0:T(8,128)(2,1)} async-done(((bf16[768,384]{1,0:T(8,128)(2,1)}), bf16[6144,384]{1,0:T(8,128)(2,1)}) %all-gather.9.cloned.1.call-update) | async-done | bytes 4718608 | tf_op jit(solution)/shard_map/all_gather | solution.py:28
  252.5 9.7 %fusion.1 = bf16[768,384]{0,1:T(8,128)(2,1)} fusion(f32[768,384]{0,1:T(8,128)S(1)} %bitcast.27, bf16[768,6144]{0,1:T(8,128)(2,1)} %bitcast.2, bf16[6144,384]{1,0:T(8,128)(2,1)} %all-gather.9.cloned.1.call-done), kind=kOutput, calls=%fused_computation.5 | convolution fusion | flops 3624468480 | bytes 15925248 | tf_op jit(solution)/shard_map/dot_general | solution.py:33
  262.2 0.0 all-gather.11.cloned.1.call-update
  262.2 0.0 copy-done.4
  262.2 0.1 dynamic_slice.14
  262.3 109.3 %all-to-all-done.1 = bf16[16,768,384]{1,2,0:T(8,128)(2,1)} async-done(((bf16[16,768,384]{1,2,0:T(8,128)(2,1)}), bf16[16,768,384]{1,2,0:T(8,128)(2,1)}, u32[]{:S(2)}, u32[]{:S(2)}) %all-to-all-start.1) | async-done | bytes 9437216 | tf_op jit(solution)/shard_map/all_to_all | solution.py:14
  371.5 0.0 all-gather.11.cloned.1.call-done
  371.5 0.0 copy-done.3
  371.5 9.8 %multiply_reduce_fusion = (f32[384]{0:T(512)S(1)}, bf16[768,384]{1,0:T(8,128)(2,1)}) fusion(bf16[768,384]{1,0:T(8,128)(2,1)S(1)} %copy-done.3, f32[768,384]{1,0:T(8,128)S(1)} %copy.9, bf16[768,6144]{0,1:T(8,128)(2,1)} %bitcast.5, bf16[6144,384]{0,1:T(8,128)(2,1)} %all-gather.11.cloned.1.call-done), kind=kOutput, calls=%fused_computation.10 | convolution fusion | flops 3625647616 | bytes 16516608 | tf_op jit(solution)/shard_map/dot_general | solution.py:33
  381.3 0.1 fusion.6
  381.5 63.2 %psum.7 = f32[32,128]{1,0:T(8,128)S(1)} all-reduce(f32[32,128]{1,0:T(8,128)S(1)} %fusion.6), channel_id=1, replica_groups=mesh['row'=8,'col'=16] {'row','col'}, use_global_device_ids=true, to_apply=%region_1.0 | all-reduce | flops 4096 | bytes 32768 | tf_op jit(solution)/shard_map/psum | solution.py:71
  444.6 0.6 constant_dynamic-slice_fusion
  (5 shorter events, 0.0 us)
Async XLA Ops:
  8.9 1.1 copy-start.1
  10.1 4.8 %copy-start = (bf16[768,384]{1,0:T(8,128)(2,1)}, bf16[768,384]{1,0:T(8,128)(2,1)S(1)}, u32[]{:S(2)}) copy-start(bf16[768,384]{1,0:T(8,128)(2,1)S(1)} %multiply_convert_fusion.1) | copy-start | bytes 1769476
  14.9 147.6 %all-to-all-start = ((bf16[16,768,384]{1,2,0:T(8,128)(2,1)}), bf16[16,768,384]{1,2,0:T(8,128)(2,1)}, u32[]{:S(2)}, u32[]{:S(2)}) async-start(bf16[16,768,384]{1,2,0:T(8,128)(2,1)} %stack.4), calls=%async_computation | async-start | bytes 18874368 | tf_op jit(solution)/shard_map/all_to_all | solution.py:14
  23.6 39.5 %all-gather.5.cloned.1.call-start = ((), (), s32[]{:S(2)}) async-start(), calls=%async_computation.2 | async-start | bytes 5308416 | tf_op jit(solution)/shard_map/all_gather | solution.py:28
  24.3 183.7 %all-gather.7.cloned.1.call-start = ((), (), s32[]{:S(2)}) async-start(), calls=%async_computation.3 | async-start | bytes 5308416 | tf_op jit(solution)/shard_map/all_gather | solution.py:28
  162.5 45.5 %copy-start.2 = (bf16[768,384]{1,0:T(8,128)(2,1)S(1)}, bf16[768,384]{1,0:T(8,128)(2,1)}, u32[]{:S(2)}) copy-start(bf16[768,384]{1,0:T(8,128)(2,1)} %param.4) | copy-start | bytes 1769476
  172.4 80.1 %all-gather.9.cloned.1.call-start = ((), (), s32[]{:S(2)}) async-start(), calls=%async_computation.4 | async-start | bytes 5308416 | tf_op jit(solution)/shard_map/all_gather | solution.py:28
  224.0 147.5 %all-to-all-start.1 = ((bf16[16,768,384]{1,2,0:T(8,128)(2,1)}), bf16[16,768,384]{1,2,0:T(8,128)(2,1)}, u32[]{:S(2)}, u32[]{:S(2)}) async-start(bf16[16,768,384]{1,2,0:T(8,128)(2,1)} %stack.5), calls=%async_computation.1 | async-start | bytes 18874368 | tf_op jit(solution)/shard_map/all_to_all | solution.py:14
  230.8 31.4 %copy-start.4 = (s32[48]{0:T(128)S(1)}, s32[48]{0:T(128)}, u32[]{:S(2)}) copy-start(s32[48]{0:T(128)} %param.7) | copy-start | bytes 580
  230.8 140.7 %copy-start.3 = (bf16[768,384]{1,0:T(8,128)(2,1)S(1)}, bf16[768,384]{1,0:T(8,128)(2,1)}, u32[]{:S(2)}) copy-start(bf16[768,384]{1,0:T(8,128)(2,1)} %param.5) | copy-start | bytes 1769476
  230.8 140.7 %all-gather.11.cloned.1.call-start = ((), (), s32[]{:S(2)}) async-start(), calls=%async_computation.5 | async-start | bytes 5308416 | tf_op jit(solution)/shard_map/all_gather | solution.py:28
Sparse Core Ops, SparseCore 0:
  26.7 36.3 all-gather.4
  172.5 35.4 all-gather.6
  218.2 34.1 all-gather.8
  262.3 34.2 all-gather.10
